TPU v7x, 32 devices: a whole 2x2x4 slice. The times are simulated.
32 devices in a mesh: dp: 4 (over y, core), tm: 8 (over z, x).
Axes of the slice: x: 2, y: 2, z: 4, core: 2. Of those that a mesh axis runs over, the one named last changes fastest.
Arguments:
- latents: bfloat16 [4, 64, 64, 1280], P('dp', 'tm'), may hold values from -6 to 6
- conv_weight: bfloat16 [1280, 3840], replicated, may hold values from -0.09375 to 0.09375
- qkv_weight: bfloat16 [1280, 1920], replicated, may hold values from -2 to 2
- out_weight: bfloat16 [640, 1280], replicated, may hold values from -0.25 to 0.25
- out_cotangent: bfloat16 [4, 32, 64, 1280], P('dp', 'tm'), may hold values from -6 to 6
Outputs:
- input_grad: bfloat16 [4, 64, 64, 1280], P('dp', 'tm')
- conv_grad: bfloat16 [1280, 3840], P('tm')
- qkv_grad: bfloat16 [1280, 1920], P('tm')
- proj_grad: bfloat16 [640, 1280], P('tm')
All inputs are finite; a program needn't handle non-finite values.
Results may differ from a plain program's by a relative error of at most 0.04.
Values may be sent and summed in bfloat16 or wider, within the bound.
A program may use at most 192 MiB of HBM per device.

v0:
```python
import math
import jax
import jax.numpy as jnp
from jax import lax
from jax.sharding import PartitionSpec as P

HEADS = 10
HEAD = 64
EPSILON = 1e-05


def from_behind(shard, axis, by):
    devices = lax.axis_size(axis)
    pairs = [(i, i + by) for i in range(devices) if 0 <= i + by < devices]
    return lax.ppermute(shard, axis, pairs)


def dot_rows(left_side, right_side):
    return jnp.dot(left_side, right_side, preferred_element_type=jnp.float32)


def column_term(lefts, right_side):
    pieces = [
        lax.dot_general(
            operand, right_side, (((0,), (0,)), ((), ())), preferred_element_type=jnp.float32
        )
        for operand in lefts
    ]
    return jnp.concatenate(pieces, axis=1)


def head_shape(packed):
    return packed.shape[:3] + (HEADS, HEAD)


def attend_forward(qkv_loc):
    width = qkv_loc.shape[-1] // 3
    shape = head_shape(qkv_loc)
    queries = qkv_loc[..., :width].reshape(shape)
    keys = qkv_loc[..., width : 2 * width].reshape(shape)
    values = qkv_loc[..., 2 * width :].reshape(shape)
    scores = jnp.einsum(
        "vqlhd,vklhd->vlhqk", queries, keys, preferred_element_type=jnp.float32
    ) / math.sqrt(HEAD)
    highest = jnp.max(scores, axis=-1, keepdims=True)
    expo = jnp.exp(scores - highest)
    probs = expo / jnp.sum(expo, axis=-1, keepdims=True)
    probs_b = probs.astype(jnp.bfloat16)
    attended = jnp.einsum(
        "vlhqk,vklhd->vqlhd", probs_b, values, preferred_element_type=jnp.float32
    ).astype(jnp.bfloat16)
    return (attended.reshape(qkv_loc.shape[:3] + (width,)), probs, probs_b)


def attend_backward(qkv_loc, attended, probs, probs_b, grad_att):
    width = qkv_loc.shape[-1] // 3
    shape = head_shape(qkv_loc)
    queries = qkv_loc[..., :width].reshape(shape)
    keys = qkv_loc[..., width : 2 * width].reshape(shape)
    values = qkv_loc[..., 2 * width :].reshape(shape)
    grad_heads = grad_att.reshape(shape)
    grad_values = jnp.einsum(
        "vlhqk,vqlhd->vklhd", probs_b, grad_heads, preferred_element_type=jnp.float32
    ).astype(jnp.bfloat16)
    grad_probs = jnp.einsum(
        "vqlhd,vklhd->vlhqk", grad_heads, values, preferred_element_type=jnp.float32
    )
    row_delta = jnp.sum(
        grad_heads.astype(jnp.float32) * attended.reshape(shape).astype(jnp.float32), axis=-1
    )
    row_delta = jnp.transpose(row_delta, (0, 2, 3, 1))[..., None]
    grad_scores = (probs * (grad_probs - row_delta) / math.sqrt(HEAD)).astype(jnp.bfloat16)
    grad_queries = jnp.einsum(
        "vlhqk,vklhd->vqlhd", grad_scores, keys, preferred_element_type=jnp.float32
    ).astype(jnp.bfloat16)
    grad_keys = jnp.einsum(
        "vlhqk,vqlhd->vklhd", grad_scores, queries, preferred_element_type=jnp.float32
    ).astype(jnp.bfloat16)
    flat_shape = qkv_loc.shape[:3] + (width,)
    return jnp.concatenate(
        [
            grad_queries.reshape(flat_shape),
            grad_keys.reshape(flat_shape),
            grad_values.reshape(flat_shape),
        ],
        axis=-1,
    )


def local(latents, conv_weight, qkv_weight, out_weight, out_cotangent):
    videos, frames, places, width = latents.shape
    half = frames // 2
    attn_width = out_weight.shape[0]
    split = latents.reshape(videos, half, 2, places, width)
    even_frames = split[:, :, 0]
    odd_frames = split[:, :, 1]
    rim_input = from_behind(odd_frames[:, half - 1 :], "tm", 1)
    prev_frames = jnp.concatenate([rim_input, odd_frames[:, : half - 1]], axis=1)
    local_rows = videos * half * places

    def as_rows(values):
        return values.reshape(local_rows, values.shape[-1])

    tap_zero = conv_weight[:, :width]
    tap_one = conv_weight[:, width : 2 * width]
    tap_two = conv_weight[:, 2 * width :]
    prev_rows = as_rows(prev_frames)
    even_rows = as_rows(even_frames)
    odd_rows = as_rows(odd_frames)
    hidden = (
        dot_rows(prev_rows, tap_zero) + dot_rows(even_rows, tap_one) + dot_rows(odd_rows, tap_two)
    ).astype(jnp.bfloat16)
    hidden_f = hidden.astype(jnp.float32)
    centred = hidden_f - jnp.mean(hidden_f, axis=-1, keepdims=True)
    inv_std = lax.rsqrt(jnp.mean(centred * centred, axis=-1, keepdims=True) + EPSILON)
    unit_rows = centred * inv_std
    normed = unit_rows.astype(jnp.bfloat16)
    qkv_rows = (
        dot_rows(normed, qkv_weight)
        .astype(jnp.bfloat16)
        .reshape(videos, half, places, 3 * attn_width)
    )
    qkv_loc = lax.all_to_all(qkv_rows, "tm", split_axis=2, concat_axis=1, tiled=True)
    attended, probs, probs_b = attend_forward(qkv_loc)
    cotangent_rows = as_rows(out_cotangent)
    attended_time = lax.all_to_all(attended, "tm", split_axis=1, concat_axis=2, tiled=True)
    grad_time = (
        dot_rows(cotangent_rows, out_weight.T)
        .astype(jnp.bfloat16)
        .reshape(videos, half, places, attn_width)
    )
    grad_att = lax.all_to_all(grad_time, "tm", split_axis=2, concat_axis=1, tiled=True)
    proj_left = as_rows(attended_time)
    grad_qkv_loc = attend_backward(qkv_loc, attended, probs, probs_b, grad_att)
    grad_qkv = as_rows(lax.all_to_all(grad_qkv_loc, "tm", split_axis=1, concat_axis=2, tiled=True))
    grad_normed = dot_rows(grad_qkv, qkv_weight.T)
    correction = (
        grad_normed
        - jnp.mean(grad_normed, axis=-1, keepdims=True)
        - unit_rows * jnp.mean(grad_normed * unit_rows, axis=-1, keepdims=True)
    )
    grad_hidden = (cotangent_rows.astype(jnp.float32) + inv_std * correction).astype(jnp.bfloat16)
    grad_four = grad_hidden.reshape(videos, half, places, width)
    rim_after = from_behind(grad_four[:, :1], "tm", -1)
    grad_next = jnp.concatenate([grad_four[:, 1:], rim_after], axis=1)
    grad_even = dot_rows(grad_hidden, tap_one.T).astype(jnp.bfloat16)
    grad_odd = (dot_rows(grad_hidden, tap_two.T) + dot_rows(as_rows(grad_next), tap_zero.T)).astype(
        jnp.bfloat16
    )
    input_grad = jnp.stack(
        [
            grad_even.reshape(videos, half, places, width),
            grad_odd.reshape(videos, half, places, width),
        ],
        axis=2,
    ).reshape(latents.shape)
    dp_count = lax.axis_size("dp")
    tm_count = lax.axis_size("tm")
    grad_scale = 1.0 / math.sqrt(dp_count * tm_count * local_rows)
    conv_part = lax.psum_scatter(
        column_term((prev_rows, even_rows, odd_rows), grad_hidden).astype(jnp.bfloat16),
        "tm",
        scatter_dimension=0,
        tiled=True,
    )
    qkv_part = lax.psum_scatter(
        column_term((normed,), grad_qkv).astype(jnp.bfloat16), "tm", scatter_dimension=0, tiled=True
    )
    proj_part = lax.psum_scatter(
        column_term((proj_left,), cotangent_rows).astype(jnp.bfloat16),
        "tm",
        scatter_dimension=0,
        tiled=True,
    )
    conv_total, qkv_total, proj_total = (
        lax.psum(conv_part, "dp").astype(jnp.float32),
        lax.psum(qkv_part, "dp").astype(jnp.float32),
        lax.psum(proj_part, "dp").astype(jnp.float32),
    )
    conv_grad = (conv_total * grad_scale).astype(jnp.bfloat16)
    qkv_grad = (qkv_total * grad_scale).astype(jnp.bfloat16)
    proj_grad = (proj_total * grad_scale).astype(jnp.bfloat16)
    return (input_grad, conv_grad, qkv_grad, proj_grad)


def solution(mesh):
    return jax.shard_map(
        local,
        mesh=mesh,
        in_specs=(P("dp", "tm", None, None), P(), P(), P(), P("dp", "tm", None, None)),
        out_specs=(P("dp", "tm", None, None), P("tm", None), P("tm", None), P("tm", None)),
        check_vma=False,
    )
```

profile of v0, /device:TPU:0, one launch (start us, length us, event | category | flops | bytes accessed | tf_op | source)
XLA Modules:
  0.0 576.1 jit_solution(3840173619625434894)
XLA Ops:
  8.6 1.8 convolution_convert_fusion.10
  11.4 7.3 %all-to-all-start.1 = ((bf16[1,4,64,640]{3,1,0,2:T(4,128)(2,1)}), bf16[1,4,64,640]{3,1,0,2:T(4,128)(2,1)S(1)}, u32[]{:S(2)}, u32[]{:S(2)}) async-start(bf16[1,4,64,640]{3,1,0,2:T(4,128)(2,1)} %copy.89), calls=%async_computation.1 | async-start | bytes 655360 | tf_op jit(solution)/shard_map/all_to_all | solution.py:132
  18.9 4.2 collective-permute-start
  23.0 2.9 fusion.5
  31.2 1.7 copy.84
  32.9 8.1 %all-to-all-start = ((bf16[1,4,64,1920]{3,1,0,2:T(4,128)(2,1)}), bf16[1,4,64,1920]{3,1,0,2:T(4,128)(2,1)}, u32[]{:S(2)}, u32[]{:S(2)}) async-start(bf16[1,4,64,1920]{3,1,0,2:T(4,128)(2,1)} %copy.84), calls=%async_computation | async-start | bytes 1966080 | tf_op jit(solution)/shard_map/all_to_all | solution.py:123
  42.9 1.8 reshape.177
  44.7 21.2 %all-to-all-done = bf16[1,4,64,1920]{3,1,0,2:T(4,128)(2,1)} async-done(((bf16[1,4,64,1920]{3,1,0,2:T(4,128)(2,1)}), bf16[1,4,64,1920]{3,1,0,2:T(4,128)(2,1)}, u32[]{:S(2)}, u32[]{:S(2)}) %all-to-all-start) | async-done | bytes 983072 | tf_op jit(solution)/shard_map/all_to_all | solution.py:123
  72.0 3.7 fusion.74
  75.7 3.2 fusion.45
  78.9 2.1 fusion.41
  85.4 1.8 reshape.168
  88.6 1.8 reshape.169
  90.4 2.4 copy.105
  92.8 1.8 reshape.170
  94.7 27.3 %all_to_all.63 = bf16[1,32,8,1920]{3,2,0,1:T(8,128)(2,1)S(1)} all-to-all(bf16[1,32,8,1920]{3,2,0,1:T(8,128)(2,1)S(1)} %maximum_bitcast_fusion), channel_id=1, replica_groups=mesh['dp'=4,'tm'=8] {'tm'}, dimensions={1} | all-to-all | bytes 1966080 | tf_op jit(solution)/shard_map/all_to_all | solution.py:135
  122.2 4.5 fusion.71
  131.0 4.4 pad_maximum_fusion
  135.5 13.7 %copy.116 = bf16[1280,3840]{1,0:T(8,128)(2,1)} copy(bf16[1280,3840]{0,1:T(8,128)(2,1)} %pad_maximum_fusion) | data formatting | bytes 19660800
  151.3 22.2 %all_to_all.64 = bf16[1,32,8,640]{3,2,0,1:T(8,128)(2,1)S(1)} all-to-all(bf16[1,32,8,640]{3,2,0,1:T(8,128)(2,1)S(1)} %bitcast.115), channel_id=1, replica_groups=mesh['dp'=4,'tm'=8] {'tm'}, dimensions={1} | all-to-all | bytes 655360 | tf_op jit(solution)/shard_map/all_to_all | solution.py:126
  173.5 1.8 convolution_convert_fusion.4
  176.6 4.0 convolution_convert_fusion
  182.2 3.0 fusion.24
  185.2 140.9 %reduce-scatter.10.cloned.1.call-done = bf16[160,3840]{1,0:T(8,128)(2,1)} async-done(((bf16[1280,3840]{1,0:T(8,128)(2,1)}), bf16[160,3840]{1,0:T(8,128)(2,1)}) %reduce-scatter.10.cloned.1.call-update) | async-done | bytes 1228816
  326.1 3.6 copy.117
  329.7 64.3 %reduce-scatter.8.cloned.1.call-done = bf16[80,1280]{1,0:T(8,128)(2,1)} async-done(((bf16[640,1280]{1,0:T(8,128)(2,1)}), bf16[80,1280]{1,0:T(8,128)(2,1)}) %reduce-scatter.8.cloned.1.call-update) | async-done | bytes 204816 | tf_op jit(solution)/shard_map/reduce_scatter | solution.py:169
  394.0 101.7 %reduce-scatter.6.cloned.1.call-done = bf16[160,1920]{1,0:T(8,128)(2,1)} async-done(((bf16[1280,1920]{1,0:T(8,128)(2,1)}), bf16[160,1920]{1,0:T(8,128)(2,1)}) %reduce-scatter.6.cloned.1.call-update) | async-done | bytes 614416 | tf_op jit(solution)/shard_map/reduce_scatter | solution.py:166
  495.7 3.0 fusion.3
  498.8 3.0 fusion.27
  503.1 57.7 %all-reduce.3.cloned.1.call-done = (bf16[160,3840]{0,1:T(8,128)(2,1)}, bf16[160,1920]{1,0:T(8,128)(2,1)}, bf16[80,1280]{1,0:T(8,128)(2,1)}) async-done(((bf16[160,3840]{0,1:T(8,128)(2,1)}, bf16[160,1920]{1,0:T(8,128)(2,1)}, bf16[80,1280]{1,0:T(8,128)(2,1)}), (bf16[160,3840]{0,1:T(8,128)(2,1)}, bf16[160,1920]{1,0:T(8,128)(2,1)}, bf16[80,1280]{1,0:T(8,128)(2,1)})) %all-reduce.3.cloned.1.call-update) | async-done | bytes 2048016 | tf_op jit(solution)/shard_map/psum | solution.py:176
  560.8 3.2 multiply_convert_fusion
  564.1 3.8 copy.112
  (100 shorter events, 33.7 us)
Async XLA Ops:
  7.2 1.4 copy-start
  10.4 8.2 %copy-start.13 = (bf16[1,8,64,1280]{3,2,1,0:T(8,128)(2,1)S(1)}, bf16[1,8,64,1280]{3,2,1,0:T(8,128)(2,1)}, u32[]{:S(2)}) copy-start(bf16[1,8,64,1280]{3,2,1,0:T(8,128)(2,1)} %param.5) | copy-start | bytes 3932164
  11.4 21.5 %all-to-all-start.1 = ((bf16[1,4,64,640]{3,1,0,2:T(4,128)(2,1)}), bf16[1,4,64,640]{3,1,0,2:T(4,128)(2,1)S(1)}, u32[]{:S(2)}, u32[]{:S(2)}) async-start(bf16[1,4,64,640]{3,1,0,2:T(4,128)(2,1)} %copy.89), calls=%async_computation.1 | async-start | bytes 655360 | tf_op jit(solution)/shard_map/all_to_all | solution.py:132
  18.6 7.4 %copy-start.14 = (bf16[1280,3840]{1,0:T(8,128)(2,1)S(1)}, bf16[1280,3840]{1,0:T(8,128)(2,1)}, u32[]{:S(2)}) copy-start(bf16[1280,3840]{1,0:T(8,128)(2,1)} %param.6) | copy-start | bytes 29491204
  18.8 7.2 %copy-start.10 = (bf16[1,4,1,64,1280]{4,3,2,1,0:T(8,128)(2,1)}, bf16[1,4,1,64,1280]{4,3,2,1,0:T(8,128)(2,1)S(1)}, u32[]{:S(2)}) copy-start(bf16[1,4,1,64,1280]{4,3,2,1,0:T(8,128)(2,1)S(1)} %get-tuple-element.31) | copy-start | bytes 1966084
  18.8 7.2 %copy-start.8 = (bf16[1,4,1,64,1280]{4,3,2,1,0:T(8,128)(2,1)}, bf16[1,4,1,64,1280]{4,3,2,1,0:T(8,128)(2,1)S(1)}, u32[]{:S(2)}) copy-start(bf16[1,4,1,64,1280]{4,3,2,1,0:T(8,128)(2,1)S(1)} %get-tuple-element.30) | copy-start | bytes 1966084
  18.9 8.2 %collective-permute-start = (bf16[1,1,64,1280]{3,2,1,0:T(8,128)(2,1)S(1)}, bf16[1,1,64,1280]{3,2,1,0:T(8,128)(2,1)S(1)}, u32[]{:S(2)}, u32[]{:S(2)}) collective-permute-start(bf16[1,1,64,1280]{3,2,1,0:T(8,128)(2,1)S(1)} %slice.52), channel_id=1, source_target_pairs={{0,1},{1,2},{2,3},{3,4},{4,5},{5,6},{6,7},{8,9},{9,10},{10,11},{11... | collective-permute-start | bytes 491528 | tf_op jit(solution)/shard_map/ppermute | solution.py:15
  27.2 2.2 slice-start
  27.2 2.4 slice-start.1
  32.9 33.0 %all-to-all-start = ((bf16[1,4,64,1920]{3,1,0,2:T(4,128)(2,1)}), bf16[1,4,64,1920]{3,1,0,2:T(4,128)(2,1)}, u32[]{:S(2)}, u32[]{:S(2)}) async-start(bf16[1,4,64,1920]{3,1,0,2:T(4,128)(2,1)} %copy.84), calls=%async_computation | async-start | bytes 1966080 | tf_op jit(solution)/shard_map/all_to_all | solution.py:123
  41.0 285.2 %reduce-scatter.10.cloned.1.call-start = ((), (), s32[]{:S(2)}) async-start(), calls=%async_computation.9 | async-start | bytes 11059200
  75.7 3.2 copy-start.12
  75.7 3.2 copy-start.16
  75.7 3.2 copy-start.19
  78.9 2.1 copy-start.15
  81.0 1.2 copy-start.4
  82.3 1.2 copy-start.5
  122.2 4.5 copy-start.2
  122.2 4.5 copy-start.6
  126.7 1.1 copy-start.11
  127.8 1.1 copy-start.9
  149.2 244.8 %reduce-scatter.8.cloned.1.call-start = ((), (), s32[]{:S(2)}) async-start(), calls=%async_computation.8 | async-start | bytes 1843200 | tf_op jit(solution)/shard_map/reduce_scatter | solution.py:169
  151.3 22.2 %copy-start.7 = (bf16[1,4,64,1280]{3,2,1,0:T(8,128)(2,1)S(1)}, bf16[1,4,64,1280]{3,2,1,0:T(8,128)(2,1)}, u32[]{:S(2)}) copy-start(bf16[1,4,64,1280]{3,2,1,0:T(8,128)(2,1)} %param.9) | copy-start | bytes 1966084
  175.4 1.2 copy-start.3
  175.4 320.3 %reduce-scatter.6.cloned.1.call-start = ((), (), s32[]{:S(2)}) async-start(), calls=%async_computation.7 | async-start | bytes 5529600 | tf_op jit(solution)/shard_map/reduce_scatter | solution.py:166
  180.6 380.3 %all-reduce.3.cloned.1.call-start = ((), (), s32[]{:S(2)}) async-start(), calls=%async_computation.10 | async-start | bytes 5570560 | tf_op jit(solution)/shard_map/psum | solution.py:176
  180.6 318.1 %collective-permute-start.1 = (bf16[1,1,64,1280]{3,2,1,0:T(8,128)(2,1)S(1)}, bf16[1,1,64,1280]{3,2,1,0:T(8,128)(2,1)S(1)}, u32[]{:S(2)}, u32[]{:S(2)}) collective-permute-start(bf16[1,1,64,1280]{3,2,1,0:T(8,128)(2,1)S(1)} %slice.59), channel_id=1, source_target_pairs={{1,0},{2,1},{3,2},{4,3},{5,4},{6,5},{7,6},{9,8},{10,9},{11,10},{12... | collective-permute-start | bytes 491528 | tf_op jit(solution)/shard_map/ppermute | solution.py:15
  564.1 3.8 copy-start.18
  564.1 4.5 copy-start.17
  564.1 5.5 copy-start.1
Sparse Core Ops, SparseCore 0:
  149.3 176.7 reduce-scatter.9
  329.6 64.3 reduce-scatter.7
  398.1 97.5 reduce-scatter.5
  498.1 62.6 all-reduce.2
where the time goes:
time: 578 us; the launch traced here: 576 us
  waiting for transfers between devices  386 us (67%)
  local copies, waits for them, and re-layouts  52.3 us (9%)
  blocking collectives  49.5 us (9%)
  matrix products  42.2 us (7%)
  starting transfers between devices  21.4 us (4%)
  between operations  14.2 us (2%)
  other arithmetic  10.5 us (2%)
    unnamed x5, waiting for transfers between devices  141 us
    reduce_scatter x1, waiting for transfers between devices, local(): lax.psum_scatter(column_term((normed,), grad_qkv).astype(jnp.bfloat16), '...  102 us
    reduce_scatter x1, waiting for transfers between devices, local(): lax.psum_scatter(column_term((proj_left,), cotangent_rows).astype(jnp.bfl...  64.3 us
    psum x1, waiting for transfers between devices, local(): lax.psum(conv_part, 'dp').astype(jnp.float32)  57.7 us
    all_to_all x1, blocking collectives, local(): lax.all_to_all(grad_qkv_loc, 'tm', split_axis=1, concat_axis=2, tiled=True)  27.3 us
    unnamed x47, local copies, waits for them, and re-layouts  26.2 us
    all_to_all x1, blocking collectives, local(): lax.all_to_all(attended, 'tm', split_axis=1, concat_axis=2, tiled=True)  22.2 us
    dot_general x9, matrix products, dot_rows(): return jnp.dot(left_side, right_side, preferred_element_type=jnp.float32)  22 us
  transfers between devices with their start and end apart: 8, of which 5 were waited for; matrix products, arithmetic and copies ran while one was open for 6% of the time, Pallas kernels for 0%

commit v1 on v0

--- a/solution.py
+++ b/solution.py
@@ -173,7 +173,7 @@
         tiled=True,
     )
     conv_total, qkv_total, proj_total = (
-        lax.psum(conv_part, "dp").astype(jnp.float32),
+        jnp.sum(lax.all_gather(conv_part, "dp"), axis=0).astype(jnp.float32),
         lax.psum(qkv_part, "dp").astype(jnp.float32),
         lax.psum(proj_part, "dp").astype(jnp.float32),
     )

time: 578 us -> 531 us (0.919)
  waiting for transfers between devices: 386 us -> 355 us
  blocking collectives: 49.5 us -> 33.4 us
  local copies, waits for them, and re-layouts: 52.3 us -> 41.7 us
  matrix products: 42.2 us -> 48.2 us
    reduce_scatter x0 -> x1, waiting for transfers between devices: none -> 172 us  [local(): lax.psum_scatter(column_term((prev_rows, even_rows, odd_rows), grad_hidde...]
    unnamed x5, waiting for transfers between devices: 141 us -> 0.08 us
    reduce_scatter x1, waiting for transfers between devices: 64.3 us -> 0.02 us  [local(): lax.psum_scatter(column_term((proj_left,), cotangent_rows).astype(jnp.bfl...]
    all_gather x0 -> x1, waiting for transfers between devices: none -> 36.5 us  [local(): lax.all_gather(conv_part, 'dp')]
    psum x1, waiting for transfers between devices: 57.7 us -> 24.2 us  [local(): lax.psum(qkv_part, 'dp').astype(jnp.float32)]
    all_to_all x1 -> x0, blocking collectives: 22.2 us -> none  [local(): lax.all_to_all(attended, 'tm', split_axis=1, concat_axis=2, tiled=True)]
    unnamed x47 -> x31, local copies, waits for them, and re-layouts: 26.2 us -> 15.1 us
    all_to_all x0 -> x1, waiting for transfers between devices: none -> 7.25 us  [local(): lax.all_to_all(attended, 'tm', split_axis=1, concat_axis=2, tiled=True)]
  transfers between devices with their start and end apart: 8 -> 10, of which waited for: 5 -> 7; matrix products, arithmetic and copies ran while one was open for 6% -> 15% of each run, Pallas kernels for 0% -> 0%
where the time goes in v1:
time: 531 us; the launch traced here: 529 us
  waiting for transfers between devices  355 us (67%)
  matrix products  48.2 us (9%)
  local copies, waits for them, and re-layouts  41.7 us (8%)
  blocking collectives  33.4 us (6%)
  starting transfers between devices  21.1 us (4%)
  other arithmetic  15.9 us (3%)
  between operations  14.2 us (3%)
    reduce_scatter x1, waiting for transfers between devices, local(): lax.psum_scatter(column_term((prev_rows, even_rows, odd_rows), grad_hidde...  172 us
    reduce_scatter x1, waiting for transfers between devices, local(): lax.psum_scatter(column_term((normed,), grad_qkv).astype(jnp.bfloat16), '...  94.8 us
    all_gather x1, waiting for transfers between devices, local(): lax.all_gather(conv_part, 'dp')  36.5 us
    all_to_all x1, blocking collectives, local(): lax.all_to_all(grad_qkv_loc, 'tm', split_axis=1, concat_axis=2, tiled=True)  33.4 us
    dot_general x9, matrix products, dot_rows(): return jnp.dot(left_side, right_side, preferred_element_type=jnp.float32)  24.6 us
    psum x1, waiting for transfers between devices, local(): lax.psum(qkv_part, 'dp').astype(jnp.float32)  24.2 us
    all_to_all x1, waiting for transfers between devices, local(): lax.all_to_all(qkv_rows, 'tm', split_axis=2, concat_axis=1, tiled=True)  19.1 us
    unnamed x31, local copies, waits for them, and re-layouts  15.1 us
  transfers between devices with their start and end apart: 10, of which 7 were waited for; matrix products, arithmetic and copies ran while one was open for 15% of the time, Pallas kernels for 0%

profile of v1, /device:TPU:0, one launch (start us, length us, event | category | flops | bytes accessed | tf_op | source)
XLA Modules:
  0.0 529.4 jit_solution(17005099139667355074)
XLA Ops:
  7.2 2.5 slice_bitcast_fusion
  10.4 4.8 collective-permute-start
  17.0 4.9 all-to-all-start.1
  21.9 3.0 fusion.5
  24.9 2.9 fusion.9
  28.0 3.2 fusion.73
  34.9 6.0 %all-to-all-start = ((bf16[1,4,64,1920]{3,1,0,2:T(4,128)(2,1)}), bf16[1,4,64,1920]{3,1,0,2:T(4,128)(2,1)S(1)}, u32[]{:S(2)}, u32[]{:S(2)}) async-start(bf16[1,4,64,1920]{3,1,0,2:T(4,128)(2,1)} %copy.83), calls=%async_computation | async-start | bytes 1966080 | tf_op jit(solution)/shard_map/all_to_all | solution.py:123
  42.8 2.7 reshape.177
  45.5 19.1 %all-to-all-done = bf16[1,4,64,1920]{3,1,0,2:T(4,128)(2,1)S(1)} async-done(((bf16[1,4,64,1920]{3,1,0,2:T(4,128)(2,1)}), bf16[1,4,64,1920]{3,1,0,2:T(4,128)(2,1)S(1)}, u32[]{:S(2)}, u32[]{:S(2)}) %all-to-all-start) | async-done | bytes 983072 | tf_op jit(solution)/shard_map/all_to_all | solution.py:123
  68.9 2.7 reshape.167
  71.6 3.4 fusion.74
  75.0 3.7 fusion.41
  80.4 3.4 all-to-all-start.3
  84.6 2.4 reshape.166
  87.0 7.2 %all-to-all-done.3 = bf16[1,32,8,640]{3,2,0,1:T(8,128)(2,1)S(1)} async-done(((bf16[1,32,8,640]{3,2,0,1:T(8,128)(2,1)}), bf16[1,32,8,640]{3,2,0,1:T(8,128)(2,1)S(1)}, u32[]{:S(2)}, u32[]{:S(2)}) %all-to-all-start.3) | async-done | bytes 327712 | tf_op jit(solution)/shard_map/all_to_all | solution.py:126
  97.4 2.8 fusion.40
  102.0 2.0 fusion.44
  105.6 2.2 fusion.45
  110.6 33.4 %all_to_all.63 = bf16[1,32,8,1920]{3,2,0,1:T(8,128)(2,1)S(1)} all-to-all(bf16[1,32,8,1920]{3,2,0,1:T(8,128)(2,1)S(1)} %maximum_bitcast_fusion), channel_id=1, replica_groups=mesh['dp'=4,'tm'=8] {'tm'}, dimensions={1} | all-to-all | bytes 1966080 | tf_op jit(solution)/shard_map/all_to_all | solution.py:135
  144.1 3.9 convolution_convert_fusion
  148.3 4.1 fusion.71
  156.3 4.4 pad_maximum_fusion
  160.7 13.7 %copy.115 = bf16[1280,3840]{1,0:T(8,128)(2,1)} copy(bf16[1280,3840]{0,1:T(8,128)(2,1)} %pad_maximum_fusion) | data formatting | bytes 19660800
  174.5 94.8 %reduce-scatter.6.cloned.1.call-done = bf16[160,1920]{1,0:T(8,128)(2,1)} async-done(((bf16[1280,1920]{1,0:T(8,128)(2,1)}), bf16[160,1920]{1,0:T(8,128)(2,1)}) %reduce-scatter.6.cloned.1.call-update) | async-done | bytes 614416 | tf_op jit(solution)/shard_map/reduce_scatter | solution.py:166
  269.3 172.3 %reduce-scatter.10.cloned.1.call-done = bf16[160,3840]{1,0:T(8,128)(2,1)} async-done(((bf16[1280,3840]{1,0:T(8,128)(2,1)}), bf16[160,3840]{1,0:T(8,128)(2,1)}) %reduce-scatter.10.cloned.1.call-update) | async-done | bytes 1228816 | tf_op jit(solution)/shard_map/reduce_scatter | solution.py:160
  443.0 3.0 fusion.24
  446.0 3.0 fusion.3
  449.6 3.0 fusion.27
  453.9 24.2 %all-reduce.3.cloned.1.call-done = (bf16[160,1920]{1,0:T(8,128)(2,1)}, bf16[80,1280]{1,0:T(8,128)(2,1)}) async-done(((bf16[160,1920]{1,0:T(8,128)(2,1)}, bf16[80,1280]{1,0:T(8,128)(2,1)}), (bf16[160,1920]{1,0:T(8,128)(2,1)}, bf16[80,1280]{1,0:T(8,128)(2,1)})) %all-reduce.3.cloned.1.call-update) | async-done | bytes 819216 | tf_op jit(solution)/shard_map/psum | solution.py:177
  479.8 2.0 multiply_convert_fusion.1
  481.7 36.5 %all-gather.3.cloned.1.call-done = bf16[640,3840]{1,0:T(8,128)(2,1)} async-done(((bf16[160,3840]{1,0:T(8,128)(2,1)}), bf16[640,3840]{1,0:T(8,128)(2,1)}) %all-gather.3.cloned.1.call-update) | async-done | bytes 4915216 | tf_op jit(solution)/shard_map/all_gather | solution.py:176
  518.3 3.4 reduce_sum.75
  (89 shorter events, 34.5 us)
Async XLA Ops:
  7.2 8.1 %copy-start = (bf16[640,1280]{1,0:T(8,128)(2,1)S(1)}, bf16[640,1280]{1,0:T(8,128)(2,1)}, u32[]{:S(2)}) copy-start(bf16[640,1280]{1,0:T(8,128)(2,1)} %param.8) | copy-start | bytes 4915204
  7.2 8.1 %copy-start.4 = (bf16[1,4,64,1280]{3,2,1,0:T(8,128)(2,1)S(1)}, bf16[1,4,64,1280]{3,2,1,0:T(8,128)(2,1)}, u32[]{:S(2)}) copy-start(bf16[1,4,64,1280]{3,2,1,0:T(8,128)(2,1)} %param.9) | copy-start | bytes 1966084
  9.7 12.2 %copy-start.8 = (bf16[1,4,1,64,1280]{4,3,2,1,0:T(8,128)(2,1)}, bf16[1,4,1,64,1280]{4,3,2,1,0:T(8,128)(2,1)S(1)}, u32[]{:S(2)}) copy-start(bf16[1,4,1,64,1280]{4,3,2,1,0:T(8,128)(2,1)S(1)} %get-tuple-element.10) | copy-start | bytes 1966084
  10.4 17.5 %collective-permute-start = (bf16[1,1,64,1280]{3,2,1,0:T(8,128)(2,1)}, bf16[1,1,64,1280]{3,2,1,0:T(8,128)(2,1)S(1)}, u32[]{:S(2)}, u32[]{:S(2)}) collective-permute-start(bf16[1,1,64,1280]{3,2,1,0:T(8,128)(2,1)} %slice.52), channel_id=1, source_target_pairs={{0,1},{1,2},{2,3},{3,4},{4,5},{5,6},{6,7},{8,9},{9,10},{10,11},{11... | collective-permute-start | bytes 491528 | tf_op jit(solution)/shard_map/ppermute | solution.py:15
  17.0 17.9 %all-to-all-start.1 = ((bf16[1,4,64,640]{3,1,0,2:T(4,128)(2,1)}), bf16[1,4,64,640]{3,1,0,2:T(4,128)(2,1)}, u32[]{:S(2)}, u32[]{:S(2)}) async-start(bf16[1,4,64,640]{3,1,0,2:T(4,128)(2,1)} %copy.88), calls=%async_computation.1 | async-start | bytes 655360 | tf_op jit(solution)/shard_map/all_to_all | solution.py:132
  21.8 3.0 copy-start.10
  28.0 3.6 slice-start
  28.0 3.6 slice-start.1
  34.9 29.7 %all-to-all-start = ((bf16[1,4,64,1920]{3,1,0,2:T(4,128)(2,1)}), bf16[1,4,64,1920]{3,1,0,2:T(4,128)(2,1)S(1)}, u32[]{:S(2)}, u32[]{:S(2)}) async-start(bf16[1,4,64,1920]{3,1,0,2:T(4,128)(2,1)} %copy.83), calls=%async_computation | async-start | bytes 1966080 | tf_op jit(solution)/shard_map/all_to_all | solution.py:123
  68.9 6.1 %copy-start.2 = (bf16[32,8,10,64]{3,2,1,0:T(8,128)(2,1)}, bf16[32,8,10,64]{3,2,1,0:T(8,128)(2,1)S(1)}, u32[]{:S(2)}) copy-start(bf16[32,8,10,64]{3,2,1,0:T(8,128)(2,1)S(1)} %reshape.164) | copy-start | bytes 983044
  80.4 13.9 %all-to-all-start.3 = ((bf16[1,32,8,640]{3,2,0,1:T(8,128)(2,1)}), bf16[1,32,8,640]{3,2,0,1:T(8,128)(2,1)S(1)}, u32[]{:S(2)}, u32[]{:S(2)}) async-start(bf16[1,32,8,640]{3,2,0,1:T(8,128)(2,1)} %bitcast.117), calls=%async_computation.4 | async-start | bytes 655360 | tf_op jit(solution)/shard_map/all_to_all | solution.py:126
  83.8 90.7 %reduce-scatter.8.cloned.1.call-start = ((), (), s32[]{:S(2)}) async-start(), calls=%async_computation.8 | async-start | bytes 1843200 | tf_op jit(solution)/shard_map/reduce_scatter | solution.py:169
  83.9 10.4 %copy-start.5 = (bf16[1,4,64,1280]{3,2,1,0:T(8,128)(2,1)S(1)}, bf16[1,4,64,1280]{3,2,1,0:T(8,128)(2,1)}, u32[]{:S(2)}) copy-start(bf16[1,4,64,1280]{3,2,1,0:T(8,128)(2,1)} %param.9) | copy-start | bytes 1966084
  96.2 1.2 copy-start.12
  96.2 173.0 %reduce-scatter.6.cloned.1.call-start = ((), (), s32[]{:S(2)}) async-start(), calls=%async_computation.7 | async-start | bytes 5529600 | tf_op jit(solution)/shard_map/reduce_scatter | solution.py:166
  97.4 2.8 copy-start.3
  100.2 0.8 copy-start.7
  148.0 293.6 %reduce-scatter.10.cloned.1.call-start = ((), (), s32[]{:S(2)}) async-start(), calls=%async_computation.10 | async-start | bytes 11059200 | tf_op jit(solution)/shard_map/reduce_scatter | solution.py:160
  148.3 4.2 copy-start.6
  153.0 1.1 copy-start.11
  154.1 1.1 copy-start.9
  174.4 303.7 %all-reduce.3.cloned.1.call-start = ((), (), s32[]{:S(2)}) async-start(), calls=%async_computation.11 | async-start | bytes 1638400 | tf_op jit(solution)/shard_map/psum | solution.py:177
  269.3 249.0 %all-gather.3.cloned.1.call-start = ((), (), s32[]{:S(2)}) async-start(), calls=%async_computation.9 | async-start | bytes 6144000 | tf_op jit(solution)/shard_map/all_gather | solution.py:176
  441.7 7.9 %collective-permute-start.1 = (bf16[1,1,64,1280]{3,2,1,0:T(8,128)(2,1)S(1)}, bf16[1,1,64,1280]{3,2,1,0:T(8,128)(2,1)S(1)}, u32[]{:S(2)}, u32[]{:S(2)}) collective-permute-start(bf16[1,1,64,1280]{3,2,1,0:T(8,128)(2,1)S(1)} %slice.59), channel_id=1, source_target_pairs={{1,0},{2,1},{3,2},{4,3},{5,4},{6,5},{7,6},{9,8},{10,9},{11,10},{12... | collective-permute-start | bytes 491528 | tf_op jit(solution)/shard_map/ppermute | solution.py:15
  518.3 4.6 copy-start.1
Sparse Core Ops, SparseCore 0:
  96.4 71.1 reduce-scatter.7
  171.7 97.5 reduce-scatter.5
  272.9 168.6 reduce-scatter.9
  444.0 34.0 all-reduce.2
  479.5 38.7 all-gather.2
